TPU v7x, 32 devices: a whole 2x2x4 slice. The times are simulated.
32 devices in a mesh: section: 4 (over y, x), student: 2 (over core), dp: 4 (over z).
Axes of the slice: x: 2, y: 2, z: 4, core: 2. Of those that a mesh axis runs over, the one named last changes fastest.
Arguments:
- in_flight: bfloat16 [4, 2, 128, 4096], P('section', 'student'), may hold values from -6 to 6
- segments: int32 [4, 2, 128], P(None, 'student'), may hold values from 0 to 3, never falling along the last dimension, each value on 1 to 64 neighbouring positions
- norm_gain: float32 [4, 4096], P('section'), may hold values from 0.5 to 1.5
- w_qkv: bfloat16 [4, 4096, 3, 1024], P('section', None, None, 'dp')
- w_out: bfloat16 [4, 1024, 4096], P('section', 'dp'), may hold values from -0.1875 to 0.1875
- final_gain: float32 [4096], replicated, may hold values from 0.25 to 1.75
- student_rows: bfloat16 [2, 3, 2, 128, 1024], P('student', None, None, 'dp'), may hold values from -6 to 6
- student_gain: float32 [2, 1024], P('student'), may hold values from 0.5 to 1.5
- w_head: bfloat16 [2, 1024, 4096], P('student', None, 'section'), may hold values from -0.1875 to 0.1875
Outputs:
- advanced: bfloat16 [4, 2, 128, 4096], P('section', 'student', 'dp')
- grad_head: float32 [2, 1024, 4096], P('student', 'dp', 'section')
Inputs may be any that keep to these rules, and one draw needn't show every extreme that they name: `segments`: along a micro-batch's tokens the crop numbers never fall; each of the 4 crops holds 1 to 64 tokens and one holds exactly 64.
All inputs are finite; a program needn't handle non-finite values.
Results may differ from a plain program's by a relative error of at most 0.025.
Values may be sent and summed in bfloat16 or wider, within the bound.
A program may use at most 64 MiB of HBM per device.

v0:
```python
import jax
import jax.numpy as jnp
from jax import lax
from jax.sharding import PartitionSpec as P

HEAD_SIZE = 128
TOK = 128


def shifted(x, axis, by):
    count = lax.axis_size(axis)
    pairs = [(i, i + by) for i in range(count) if 0 <= i + by < count]
    return lax.ppermute(x, axis, pairs)


def broadcast(value, axis, source):
    kept = jnp.where(lax.axis_index(axis) == source, value, 0).astype(value.dtype)
    return lax.psum(kept, axis)


def layer_norm(rows, gain):
    rows = rows.astype(jnp.float32)
    centred = rows - jnp.mean(rows, axis=-1, keepdims=True)
    spread = jnp.mean(centred * centred, axis=-1, keepdims=True)
    return centred * lax.rsqrt(spread + 1e-06) * gain


def attend(state, crops, gain, weights_qkv, weights_out):
    tokens = state.shape[0]
    width = weights_out.shape[0]
    heads = width // HEAD_SIZE
    normed = layer_norm(state, gain).astype(jnp.bfloat16)
    qkv = jnp.dot(normed, weights_qkv, preferred_element_type=jnp.float32).astype(jnp.bfloat16)
    query = qkv[:, :width].reshape(tokens, heads, HEAD_SIZE)
    keys = qkv[:, width : 2 * width].reshape(tokens, heads, HEAD_SIZE)
    values = qkv[:, 2 * width :].reshape(tokens, heads, HEAD_SIZE)
    scores = jnp.einsum(
        "qhd,khd->hqk", query, keys, preferred_element_type=jnp.float32
    ) * HEAD_SIZE ** (-0.5)
    same = crops[:, None] == crops[None, :]
    scores = jnp.where(same[None], scores, -1e30)
    top = jnp.max(scores, axis=-1, keepdims=True)
    expo = jnp.exp(scores - top)
    probs = (expo / jnp.sum(expo, axis=-1, keepdims=True)).astype(jnp.bfloat16)
    mixed = jnp.einsum("hqk,khd->qhd", probs, values, preferred_element_type=jnp.float32).astype(
        jnp.bfloat16
    )
    return jnp.dot(mixed.reshape(tokens, width), weights_out, preferred_element_type=jnp.float32)


def on_device(
    in_flight, segments, norm_gain, w_qkv, w_out, final_gain, student_rows, student_gain, w_head
):
    section = lax.axis_index("section")
    root = lax.axis_size("section") - 1
    share = in_flight.shape[2] // lax.axis_size("dp")
    first_row = lax.axis_index("dp") * share
    ticks = student_rows.shape[1]
    model_width = in_flight.shape[3]
    weights_qkv = w_qkv[0].reshape(model_width, -1)
    weights_out = w_out[0]
    gain = norm_gain[0]
    crop_table = segments[:, 0, :]
    finals = []
    whole = in_flight[0, 0]
    own_rows = lax.dynamic_slice_in_dim(whole, first_row, share, 0)
    for tick in range(ticks):
        if tick > 0:
            whole = lax.all_gather(own_rows, "dp", axis=0, tiled=True)
        crops = lax.dynamic_index_in_dim(crop_table, section - tick, 0, keepdims=False)
        partial_value = attend(whole, crops, gain, weights_qkv, weights_out)
        summed = lax.psum_scatter(
            partial_value.astype(jnp.bfloat16), "dp", scatter_dimension=0, tiled=True
        ).astype(jnp.float32)
        own_rows = (own_rows.astype(jnp.float32) + summed).astype(jnp.bfloat16)
        finals.append(layer_norm(own_rows, final_gain).astype(jnp.bfloat16))
        own_rows = shifted(own_rows, "section", 1)
    advanced = own_rows[None, None]
    finished = jnp.stack(finals)[:, None]
    block = w_head.shape[2]
    block_start = section * block
    columns = lax.all_gather(finished, "student", axis=1, tiled=True)
    spread_rows = broadcast(columns, "section", root)
    targets = lax.dynamic_slice_in_dim(spread_rows, block_start, block, 3)
    student_width = student_rows.shape[4]
    feats = (
        layer_norm(student_rows[0], student_gain[0]).astype(jnp.bfloat16).reshape(-1, student_width)
    )
    pred = jnp.dot(feats, w_head[0], preferred_element_type=jnp.float32)
    err = ((pred - targets.reshape(-1, block).astype(jnp.float32)) * (2.0 / TOK)).astype(
        jnp.bfloat16
    )
    term = lax.dot_general(feats, err, (((0,), (0,)), ((), ())), preferred_element_type=jnp.float32)
    grad = lax.psum_scatter(
        term.astype(jnp.bfloat16), "dp", scatter_dimension=0, tiled=True
    ).astype(jnp.float32)
    return (advanced, grad[None])


def solution(mesh):
    in_specs = (
        P("section", "student", None, None),
        P(None, "student", None),
        P("section", None),
        P("section", None, None, "dp"),
        P("section", "dp", None),
        P(),
        P("student", None, None, "dp", None),
        P("student", None),
        P("student", None, "section"),
    )
    out_specs = (P("section", "student", "dp", None), P("student", "dp", "section"))
    return jax.shard_map(
        on_device, mesh=mesh, in_specs=in_specs, out_specs=out_specs, check_vma=False
    )
```

profile of v0, /device:TPU:0, one launch (start us, length us, event | category | flops | bytes accessed | tf_op | source)
XLA Modules:
  0.0 340.8 jit_solution(15224556704318031938)
XLA Ops:
  8.2 8.9 %copy.23 = bf16[1,4096,3,256]{1,3,2,0:T(8,128)(2,1)} copy(bf16[1,4096,3,256]{3,1,2,0:T(8,128)(2,1)} %param.12) | data formatting | bytes 12582912 | tf_op args[3]
  17.8 5.0 %convolution_convert_fusion.6 = bf16[128,768]{1,0:T(8,128)(2,1)S(1)} fusion(bf16[4096,768]{0,1:T(8,128)(2,1)} %bitcast.129, bf16[1,1,128,4096]{3,2,1,0:T(8,128)(2,1)S(1)} %copy-done.2, f32[4096]{0:T(1024)S(1)} %bitcast.144, f32[128]{0:T(128)S(1)} %add_rsqrt_fusion.6, f32[128]{0:T(128)S(1)} %broadcast_multiply_fusion.6), kind=kOutput, calls=%fused_computation.41 | convolution fusion | flops 808026112 | bytes 7554048 | tf_op jit(solution)/shard_map/dot_general | solution.py:33
  23.4 1.4 convolution_convert_fusion.2
  24.9 30.1 %reduce-scatter.5.cloned.1.call-done = bf16[32,4096]{1,0:T(8,128)(2,1)} async-done(((bf16[128,4096]{1,0:T(8,128)(2,1)}), bf16[32,4096]{1,0:T(8,128)(2,1)}) %reduce-scatter.5.cloned.1.call-update) | async-done | bytes 262160 | tf_op jit(solution)/shard_map/reduce_scatter | solution.py:72
  55.0 1.1 convert_reduce_fusion.5
  56.1 3.4 collective-permute-start
  59.5 5.1 %collective-permute-done = bf16[32,4096]{1,0:T(8,128)(2,1)S(1)} collective-permute-done((bf16[32,4096]{1,0:T(8,128)(2,1)S(1)}, bf16[32,4096]{1,0:T(8,128)(2,1)S(1)}, u32[]{:S(2)}, u32[]{:S(2)}) %collective-permute-start) | collective-permute-done | bytes 262176 | tf_op jit(solution)/shard_map/ppermute | solution.py:13
  65.6 27.8 %all-gather.5.cloned.1.call-done = bf16[128,4096]{1,0:T(8,128)(2,1)} async-done(((bf16[32,4096]{1,0:T(8,128)(2,1)}), bf16[128,4096]{1,0:T(8,128)(2,1)}) %all-gather.5.cloned.1.call-update) | async-done | bytes 1048592 | tf_op jit(solution)/shard_map/all_gather | solution.py:69
  93.4 1.5 convert_reduce_fusion.2
  95.0 1.7 fusion.10
  96.6 5.0 %convolution_convert_fusion.5 = bf16[128,768]{1,0:T(8,128)(2,1)S(1)} fusion(bf16[4096,768]{0,1:T(8,128)(2,1)} %bitcast.130, bf16[128,4096]{1,0:T(8,128)(2,1)S(1)} %copy-done.3, f32[4096]{0:T(1024)S(1)} %bitcast.145, f32[128]{0:T(128)S(1)} %add_rsqrt_fusion.5, f32[128]{0:T(128)S(1)} %broadcast_multiply_fusion.5), kind=kOutput, calls=%fused_computation.40 | convolution fusion | flops 808026112 | bytes 7554048 | tf_op jit(solution)/shard_map/dot_general | solution.py:33
  102.2 1.4 convolution_convert_fusion.1
  103.8 26.8 %reduce-scatter.7.cloned.1.call-done = bf16[32,4096]{1,0:T(8,128)(2,1)} async-done(((bf16[128,4096]{1,0:T(8,128)(2,1)}), bf16[32,4096]{1,0:T(8,128)(2,1)}) %reduce-scatter.7.cloned.1.call-update) | async-done | bytes 262160 | tf_op jit(solution)/shard_map/reduce_scatter | solution.py:72
  130.5 1.1 convert_reduce_fusion.4
  131.7 3.4 collective-permute-start.1
  135.1 5.1 %collective-permute-done.1 = bf16[32,4096]{1,0:T(8,128)(2,1)S(1)} collective-permute-done((bf16[32,4096]{1,0:T(8,128)(2,1)S(1)}, bf16[32,4096]{1,0:T(8,128)(2,1)S(1)}, u32[]{:S(2)}, u32[]{:S(2)}) %collective-permute-start.1) | collective-permute-done | bytes 262176 | tf_op jit(solution)/shard_map/ppermute | solution.py:13
  141.0 27.9 %all-gather.7.cloned.1.call-done = bf16[128,4096]{1,0:T(8,128)(2,1)} async-done(((bf16[32,4096]{1,0:T(8,128)(2,1)}), bf16[128,4096]{1,0:T(8,128)(2,1)}) %all-gather.7.cloned.1.call-update) | async-done | bytes 1048592 | tf_op jit(solution)/shard_map/all_gather | solution.py:69
  168.9 1.5 convert_reduce_fusion.1
  170.5 1.7 fusion.7
  172.1 5.0 %convolution_convert_fusion.4 = bf16[128,768]{1,0:T(8,128)(2,1)S(1)} fusion(bf16[4096,768]{0,1:T(8,128)(2,1)} %bitcast.131, bf16[128,4096]{1,0:T(8,128)(2,1)S(1)} %copy-done.4, f32[128]{0:T(128)S(1)} %add_rsqrt_fusion.4, f32[128]{0:T(128)S(1)} %broadcast_multiply_fusion.4, f32[4096]{0:T(1024)S(1)} %bitcast.146), kind=kOutput, calls=%fused_computation.39 | convolution fusion | flops 808026112 | bytes 7554048 | tf_op jit(solution)/shard_map/dot_general | solution.py:33
  177.7 1.4 convolution_convert_fusion
  179.8 26.2 %reduce-scatter.9.cloned.1.call-done = bf16[32,4096]{1,0:T(8,128)(2,1)} async-done(((bf16[128,4096]{1,0:T(8,128)(2,1)}), bf16[32,4096]{1,0:T(8,128)(2,1)}) %reduce-scatter.9.cloned.1.call-update) | async-done | bytes 262160 | tf_op jit(solution)/shard_map/reduce_scatter | solution.py:72
  206.0 1.1 convert_reduce_fusion.3
  208.8 8.4 %all-gather.9.cloned.1.call-done = bf16[3,64,4096]{2,1,0:T(8,128)(2,1)} async-done(((bf16[3,32,4096]{2,1,0:T(8,128)(2,1)}), bf16[3,64,4096]{2,1,0:T(8,128)(2,1)}) %all-gather.9.cloned.1.call-update) | async-done | bytes 1572880 | tf_op jit(solution)/shard_map/all_gather | solution.py:82
  217.2 1.3 broadcast_select_fusion
  219.7 62.6 %all-reduce.2.cloned.1.call-done = bf16[3,2,32,4096]{3,2,1,0:T(8,128)(2,1)} async-done(((bf16[3,2,32,4096]{3,2,1,0:T(8,128)(2,1)}), bf16[3,2,32,4096]{3,2,1,0:T(8,128)(2,1)}) %all-reduce.2.cloned.1.call-update) | async-done | bytes 1572880 | tf_op jit(solution)/shard_map/psum | solution.py:18
  282.3 1.0 constant_dynamic-slice_fusion
  283.3 4.1 %convolution_convert_fusion.3 = bf16[1024,1024]{1,0:T(8,128)(2,1)} fusion(bf16[192,1024]{1,0:T(8,128)(2,1)S(1)} %fusion.62, bf16[192,1024]{1,0:T(8,128)(2,1)S(1)} %bitcast.133, bf16[1,1024,1024]{2,1,0:T(8,128)(2,1)} %param.17, bf16[192,1024]{1,0:T(8,128)(2,1)S(1)} %bitcast.134), kind=kOutput, calls=%fused_computation.34 | convolution fusion | flops 807141376 | bytes 5373952 | tf_op jit(solution)/shard_map/dot_general | solution.py:93
  287.4 3.4 collective-permute-start.2
  290.8 5.4 %collective-permute-done.2 = bf16[32,4096]{1,0:T(8,128)(2,1)S(1)} collective-permute-done((bf16[32,4096]{1,0:T(8,128)(2,1)S(1)}, bf16[32,4096]{1,0:T(8,128)(2,1)S(1)}, u32[]{:S(2)}, u32[]{:S(2)}) %collective-permute-start.2) | collective-permute-done | bytes 262176 | tf_op jit(solution)/shard_map/ppermute | solution.py:13
  296.1 35.0 %reduce-scatter.11.cloned.1.call-done = bf16[256,1024]{1,0:T(8,128)(2,1)} async-done(((bf16[1024,1024]{1,0:T(8,128)(2,1)}), bf16[256,1024]{1,0:T(8,128)(2,1)}) %reduce-scatter.11.cloned.1.call-update) | async-done | bytes 524304 | tf_op jit(solution)/shard_map/reduce_scatter | solution.py:94
  331.2 2.1 bitcast_convert_fusion
  (86 shorter events, 9.2 us)
Async XLA Ops:
  7.2 16.2 %copy-start = (bf16[1,256,4096]{2,1,0:T(8,128)(2,1)S(1)}, bf16[1,256,4096]{2,1,0:T(8,128)(2,1)}, u32[]{:S(2)}) copy-start(bf16[1,256,4096]{2,1,0:T(8,128)(2,1)} %param.13) | copy-start | bytes 6291460
  7.2 47.8 %reduce-scatter.5.cloned.1.call-start = ((), (), s32[]{:S(2)}) async-start(), calls=%async_computation.4 | async-start | bytes 1310720 | tf_op jit(solution)/shard_map/reduce_scatter | solution.py:72
  8.2 8.9 %copy-start.2 = (bf16[1,1,128,4096]{3,2,1,0:T(8,128)(2,1)S(1)}, bf16[1,1,128,4096]{3,2,1,0:T(8,128)(2,1)}, u32[]{:S(2)}) copy-start(bf16[1,1,128,4096]{3,2,1,0:T(8,128)(2,1)} %param.9) | copy-start | bytes 3145732
  17.1 0.7 copy-start.11
  24.9 68.6 %all-gather.5.cloned.1.call-start = ((), (), s32[]{:S(2)}) async-start(), calls=%async_computation.5 | async-start | bytes 1310720 | tf_op jit(solution)/shard_map/all_gather | solution.py:69
  56.1 8.5 %collective-permute-start = (bf16[32,4096]{1,0:T(8,128)(2,1)S(1)}, bf16[32,4096]{1,0:T(8,128)(2,1)S(1)}, u32[]{:S(2)}, u32[]{:S(2)}) collective-permute-start(bf16[32,4096]{1,0:T(8,128)(2,1)S(1)} %get-tuple-element.3), channel_id=1, source_target_pairs={{0,8},{8,16},{16,24},{1,9},{9,17},{17,25},{2,10},{10,18},{18,26},{... | collective-permute-start | bytes 786440 | tf_op jit(solution)/shard_map/ppermute | solution.py:13
  64.7 0.7 copy-start.7
  65.4 65.1 %reduce-scatter.7.cloned.1.call-start = ((), (), s32[]{:S(2)}) async-start(), calls=%async_computation.6 | async-start | bytes 1310720 | tf_op jit(solution)/shard_map/reduce_scatter | solution.py:72
  93.4 3.2 copy-start.3
  102.2 28.3 %copy-start.8 = (bf16[32,4096]{1,0:T(8,128)(2,1)S(1)}, bf16[32,4096]{1,0:T(8,128)(2,1)}, u32[]{:S(2)}) copy-start(bf16[32,4096]{1,0:T(8,128)(2,1)} %copy-done.7) | copy-start | bytes 786436
  103.7 65.2 %all-gather.7.cloned.1.call-start = ((), (), s32[]{:S(2)}) async-start(), calls=%async_computation.7 | async-start | bytes 1310720 | tf_op jit(solution)/shard_map/all_gather | solution.py:69
  131.7 8.5 %collective-permute-start.1 = (bf16[32,4096]{1,0:T(8,128)(2,1)S(1)}, bf16[32,4096]{1,0:T(8,128)(2,1)S(1)}, u32[]{:S(2)}, u32[]{:S(2)}) collective-permute-start(bf16[32,4096]{1,0:T(8,128)(2,1)S(1)} %get-tuple-element.5), channel_id=1, source_target_pairs={{0,8},{8,16},{16,24},{1,9},{9,17},{17,25},{2,10},{10,18},{18,26},{... | collective-permute-start | bytes 786440 | tf_op jit(solution)/shard_map/ppermute | solution.py:13
  140.2 0.7 copy-start.5
  140.9 65.1 %reduce-scatter.9.cloned.1.call-start = ((), (), s32[]{:S(2)}) async-start(), calls=%async_computation.8 | async-start | bytes 1310720 | tf_op jit(solution)/shard_map/reduce_scatter | solution.py:72
  168.9 3.2 copy-start.4
  177.7 28.3 %copy-start.6 = (bf16[32,4096]{1,0:T(8,128)(2,1)S(1)}, bf16[32,4096]{1,0:T(8,128)(2,1)}, u32[]{:S(2)}) copy-start(bf16[32,4096]{1,0:T(8,128)(2,1)} %copy-done.5) | copy-start | bytes 786436
  179.2 28.3 %copy-start.9 = (f32[4096]{0:T(1024)S(1)}, f32[4096]{0:T(1024)}, u32[]{:S(2)}) copy-start(f32[4096]{0:T(1024)} %param.14) | copy-start | bytes 49156
  179.2 38.0 %all-gather.9.cloned.1.call-start = ((), (), s32[]{:S(2)}) async-start(), calls=%async_computation.11 | async-start | bytes 2359296 | tf_op jit(solution)/shard_map/all_gather | solution.py:82
  208.8 73.5 %all-reduce.2.cloned.1.call-start = ((), (), s32[]{:S(2)}) async-start(), calls=%async_computation.9 | async-start | bytes 3145728 | tf_op jit(solution)/shard_map/psum | solution.py:18
  208.8 9.7 %copy-start.1 = (bf16[1,3,2,32,1024]{4,3,2,1,0:T(8,128)(2,1)S(1)}, bf16[1,3,2,32,1024]{4,3,2,1,0:T(8,128)(2,1)}, u32[]{:S(2)}) copy-start(bf16[1,3,2,32,1024]{4,3,2,1,0:T(8,128)(2,1)} %param.15) | copy-start | bytes 1179652
  208.8 10.3 %copy-start.10 = (f32[1,1024]{1,0:T(1,128)S(1)}, f32[1,1024]{1,0:T(1,128)}, u32[]{:S(2)}) copy-start(f32[1,1024]{1,0:T(1,128)} %param.16) | copy-start | bytes 12292
  218.5 112.7 %reduce-scatter.11.cloned.1.call-start = ((), (), s32[]{:S(2)}) async-start(), calls=%async_computation.10 | async-start | bytes 2621440 | tf_op jit(solution)/shard_map/reduce_scatter | solution.py:94
  287.4 8.8 %collective-permute-start.2 = (bf16[32,4096]{1,0:T(8,128)(2,1)S(1)}, bf16[32,4096]{1,0:T(8,128)(2,1)S(1)}, u32[]{:S(2)}, u32[]{:S(2)}) collective-permute-start(bf16[32,4096]{1,0:T(8,128)(2,1)S(1)} %get-tuple-element.7), channel_id=1, source_target_pairs={{0,8},{8,16},{16,24},{1,9},{9,17},{17,25},{2,10},{10,18},{18,26},{... | collective-permute-start | bytes 786440 | tf_op jit(solution)/shard_map/ppermute | solution.py:13
Sparse Core Ops, SparseCore 0:
  25.0 29.9 reduce-scatter.4
  65.5 27.8 all-gather.4
  103.8 26.6 reduce-scatter.6
  141.1 27.8 all-gather.6
  179.3 26.6 reduce-scatter.8
  208.9 8.2 all-gather.8
  220.3 61.9 all-reduce.1
  287.5 43.6 reduce-scatter.10
where the time goes:
time: 342 us; the launch traced here: 341 us
  waiting for transfers between devices  261 us (76%)
  matrix products  24.5 us (7%)
  other arithmetic  17.2 us (5%)
  between operations  14.5 us (4%)
  local copies, waits for them, and re-layouts  13.5 us (4%)
  starting transfers between devices  10.5 us (3%)
    reduce_scatter x3, waiting for transfers between devices, on_device(): lax.psum_scatter(partial_value.astype(jnp.bfloat16), 'dp', scatter_dimens...  83.1 us
    psum x1, waiting for transfers between devices, broadcast(): return lax.psum(kept, axis)  62.6 us
    all_gather x2, waiting for transfers between devices, on_device(): whole = lax.all_gather(own_rows, 'dp', axis=0, tiled=True)  55.8 us
    reduce_scatter x1, waiting for transfers between devices, on_device(): lax.psum_scatter(term.astype(jnp.bfloat16), 'dp', scatter_dimension=0, ti...  35 us
    ppermute x3, waiting for transfers between devices, shifted(): return lax.ppermute(x, axis, pairs)  15.6 us
    dot_general x3, matrix products, attend(): jnp.dot(normed, weights_qkv, preferred_element_type=jnp.float32)  15.1 us
    unnamed x29, local copies, waits for them, and re-layouts  11.1 us
    ppermute x3, starting transfers between devices, shifted(): return lax.ppermute(x, axis, pairs)  10.2 us
  transfers between devices with their start and end apart: 11, of which 11 were waited for; matrix products, arithmetic and copies ran while one was open for 0% of the time, Pallas kernels for 0%

commit v1 on v0

--- a/solution.py
+++ b/solution.py
@@ -15,7 +15,7 @@
 
 def broadcast(value, axis, source):
     kept = jnp.where(lax.axis_index(axis) == source, value, 0).astype(value.dtype)
-    return lax.psum(kept, axis)
+    return jnp.sum(lax.all_gather(kept, axis), axis=0)
 
 
 def layer_norm(rows, gain):

time: 342 us -> 356 us (1.041)
  waiting for transfers between devices: 261 us -> 269 us
  other arithmetic: 17.2 us -> 22.8 us
    all_gather x0 -> x1, waiting for transfers between devices: none -> 71.4 us  [broadcast(): return jnp.sum(lax.all_gather(kept, axis), axis=0)]
    psum x1 -> x0, waiting for transfers between devices: 62.6 us -> none  [broadcast(): return lax.psum(kept, axis)]
    reduce_sum x0 -> x1, other arithmetic: none -> 5.58 us  [broadcast(): return jnp.sum(lax.all_gather(kept, axis), axis=0)]
where the time goes in v1:
time: 356 us; the launch traced here: 355 us
  waiting for transfers between devices  269 us (76%)
  matrix products  24.5 us (7%)
  other arithmetic  22.8 us (6%)
  between operations  14.5 us (4%)
  local copies, waits for them, and re-layouts  13.5 us (4%)
  starting transfers between devices  10.7 us (3%)
    reduce_scatter x3, waiting for transfers between devices, on_device(): lax.psum_scatter(partial_value.astype(jnp.bfloat16), 'dp', scatter_dimens...  83.1 us
    all_gather x1, waiting for transfers between devices, broadcast(): return jnp.sum(lax.all_gather(kept, axis), axis=0)  71.4 us
    all_gather x2, waiting for transfers between devices, on_device(): whole = lax.all_gather(own_rows, 'dp', axis=0, tiled=True)  55.8 us
    reduce_scatter x1, waiting for transfers between devices, on_device(): lax.psum_scatter(term.astype(jnp.bfloat16), 'dp', scatter_dimension=0, ti...  35 us
    ppermute x3, waiting for transfers between devices, shifted(): return lax.ppermute(x, axis, pairs)  15.6 us
    dot_general x3, matrix products, attend(): jnp.dot(normed, weights_qkv, preferred_element_type=jnp.float32)  15.1 us
    unnamed x29, local copies, waits for them, and re-layouts  11.1 us
    ppermute x3, starting transfers between devices, shifted(): return lax.ppermute(x, axis, pairs)  10.2 us
  transfers between devices with their start and end apart: 11, of which 11 were waited for; matrix products, arithmetic and copies ran while one was open for 0% of the time, Pallas kernels for 0%

profile of v1, /device:TPU:0, one launch (start us, length us, event | category | flops | bytes accessed | tf_op | source)
XLA Modules:
  0.0 355.4 jit_solution(2201067134488568034)
XLA Ops:
  8.2 8.9 %copy.36 = bf16[1,4096,3,256]{1,3,2,0:T(8,128)(2,1)} copy(bf16[1,4096,3,256]{3,1,2,0:T(8,128)(2,1)} %param.12) | data formatting | bytes 12582912 | tf_op args[3]
  17.8 5.0 %convolution_convert_fusion.6 = bf16[128,768]{1,0:T(8,128)(2,1)S(1)} fusion(bf16[4096,768]{0,1:T(8,128)(2,1)} %bitcast.130, bf16[1,1,128,4096]{3,2,1,0:T(8,128)(2,1)S(1)} %copy-done.2, f32[4096]{0:T(1024)S(1)} %bitcast.146, f32[128]{0:T(128)S(1)} %add_rsqrt_fusion.6, f32[128]{0:T(128)S(1)} %broadcast_multiply_fusion.6), kind=kOutput, calls=%fused_computation.41 | convolution fusion | flops 808026112 | bytes 7554048 | tf_op jit(solution)/shard_map/dot_general | solution.py:33
  23.4 1.4 convolution_convert_fusion.2
  24.9 30.1 %reduce-scatter.5.cloned.1.call-done = bf16[32,4096]{1,0:T(8,128)(2,1)} async-done(((bf16[128,4096]{1,0:T(8,128)(2,1)}), bf16[32,4096]{1,0:T(8,128)(2,1)}) %reduce-scatter.5.cloned.1.call-update) | async-done | bytes 262160 | tf_op jit(solution)/shard_map/reduce_scatter | solution.py:72
  55.0 1.1 convert_reduce_fusion.5
  56.1 3.4 collective-permute-start
  59.5 5.1 %collective-permute-done = bf16[32,4096]{1,0:T(8,128)(2,1)S(1)} collective-permute-done((bf16[32,4096]{1,0:T(8,128)(2,1)S(1)}, bf16[32,4096]{1,0:T(8,128)(2,1)S(1)}, u32[]{:S(2)}, u32[]{:S(2)}) %collective-permute-start) | collective-permute-done | bytes 262176 | tf_op jit(solution)/shard_map/ppermute | solution.py:13
  65.6 27.8 %all-gather.7.cloned.1.call-done = bf16[128,4096]{1,0:T(8,128)(2,1)} async-done(((bf16[32,4096]{1,0:T(8,128)(2,1)}), bf16[128,4096]{1,0:T(8,128)(2,1)}) %all-gather.7.cloned.1.call-update) | async-done | bytes 1048592 | tf_op jit(solution)/shard_map/all_gather | solution.py:69
  93.4 1.5 convert_reduce_fusion.2
  95.0 1.7 fusion.10
  96.6 5.0 %convolution_convert_fusion.5 = bf16[128,768]{1,0:T(8,128)(2,1)S(1)} fusion(bf16[4096,768]{0,1:T(8,128)(2,1)} %bitcast.131, bf16[128,4096]{1,0:T(8,128)(2,1)S(1)} %copy-done.3, f32[4096]{0:T(1024)S(1)} %bitcast.147, f32[128]{0:T(128)S(1)} %add_rsqrt_fusion.5, f32[128]{0:T(128)S(1)} %broadcast_multiply_fusion.5), kind=kOutput, calls=%fused_computation.40 | convolution fusion | flops 808026112 | bytes 7554048 | tf_op jit(solution)/shard_map/dot_general | solution.py:33
  102.2 1.4 convolution_convert_fusion.1
  103.8 26.7 %reduce-scatter.7.cloned.1.call-done = bf16[32,4096]{1,0:T(8,128)(2,1)} async-done(((bf16[128,4096]{1,0:T(8,128)(2,1)}), bf16[32,4096]{1,0:T(8,128)(2,1)}) %reduce-scatter.7.cloned.1.call-update) | async-done | bytes 262160 | tf_op jit(solution)/shard_map/reduce_scatter | solution.py:72
  130.5 1.1 convert_reduce_fusion.4
  131.6 3.4 collective-permute-start.1
  135.1 5.1 %collective-permute-done.1 = bf16[32,4096]{1,0:T(8,128)(2,1)S(1)} collective-permute-done((bf16[32,4096]{1,0:T(8,128)(2,1)S(1)}, bf16[32,4096]{1,0:T(8,128)(2,1)S(1)}, u32[]{:S(2)}, u32[]{:S(2)}) %collective-permute-start.1) | collective-permute-done | bytes 262176 | tf_op jit(solution)/shard_map/ppermute | solution.py:13
  141.0 27.9 %all-gather.9.cloned.1.call-done = bf16[128,4096]{1,0:T(8,128)(2,1)} async-done(((bf16[32,4096]{1,0:T(8,128)(2,1)}), bf16[128,4096]{1,0:T(8,128)(2,1)}) %all-gather.9.cloned.1.call-update) | async-done | bytes 1048592 | tf_op jit(solution)/shard_map/all_gather | solution.py:69
  168.9 1.5 convert_reduce_fusion.1
  170.5 1.7 fusion.7
  172.1 5.0 %convolution_convert_fusion.4 = bf16[128,768]{1,0:T(8,128)(2,1)S(1)} fusion(bf16[4096,768]{0,1:T(8,128)(2,1)} %bitcast.132, bf16[128,4096]{1,0:T(8,128)(2,1)S(1)} %copy-done.4, f32[128]{0:T(128)S(1)} %add_rsqrt_fusion.4, f32[128]{0:T(128)S(1)} %broadcast_multiply_fusion.4, f32[4096]{0:T(1024)S(1)} %bitcast.148), kind=kOutput, calls=%fused_computation.39 | convolution fusion | flops 808026112 | bytes 7554048 | tf_op jit(solution)/shard_map/dot_general | solution.py:33
  177.7 1.4 convolution_convert_fusion
  179.8 26.2 %reduce-scatter.9.cloned.1.call-done = bf16[32,4096]{1,0:T(8,128)(2,1)} async-done(((bf16[128,4096]{1,0:T(8,128)(2,1)}), bf16[32,4096]{1,0:T(8,128)(2,1)}) %reduce-scatter.9.cloned.1.call-update) | async-done | bytes 262160 | tf_op jit(solution)/shard_map/reduce_scatter | solution.py:72
  206.0 1.1 convert_reduce_fusion.3
  208.8 8.4 %all-gather.11.cloned.1.call-done = bf16[3,64,4096]{2,1,0:T(8,128)(2,1)} async-done(((bf16[3,32,4096]{2,1,0:T(8,128)(2,1)}), bf16[3,64,4096]{2,1,0:T(8,128)(2,1)}) %all-gather.11.cloned.1.call-update) | async-done | bytes 1572880 | tf_op jit(solution)/shard_map/all_gather | solution.py:82
  217.2 1.3 broadcast_select_fusion
  219.8 71.4 %all-gather.13.cloned.1.call-done = bf16[12,2,32,4096]{3,2,1,0:T(8,128)(2,1)} async-done(((bf16[3,2,32,4096]{3,2,1,0:T(8,128)(2,1)}), bf16[12,2,32,4096]{3,2,1,0:T(8,128)(2,1)}) %all-gather.13.cloned.1.call-update) | async-done | bytes 6291472 | tf_op jit(solution)/shard_map/all_gather | solution.py:18
  291.2 5.6 %reduce_sum.182 = bf16[3,2,32,4096]{3,2,1,0:T(8,128)(2,1)} reduce(bf16[4,3,2,32,4096]{4,3,2,1,0:T(8,128)(2,1)} %bitcast.133, bf16[]{:T(256)} %constant.73.clone.1), dimensions={0}, to_apply=%region_23.24 | reduce | flops 2359296 | bytes 7864322 | tf_op jit(solution)/shard_map/reduce_sum | solution.py:18
  297.8 4.1 %convolution_convert_fusion.3 = bf16[1024,1024]{1,0:T(8,128)(2,1)} fusion(bf16[192,1024]{1,0:T(8,128)(2,1)S(1)} %fusion.62, bf16[192,1024]{1,0:T(8,128)(2,1)S(1)} %bitcast.135, bf16[1,1024,1024]{2,1,0:T(8,128)(2,1)} %param.17, bf16[192,1024]{1,0:T(8,128)(2,1)S(1)} %bitcast.136), kind=kOutput, calls=%fused_computation.34 | convolution fusion | flops 807141376 | bytes 5373952 | tf_op jit(solution)/shard_map/dot_general | solution.py:93
  302.0 3.4 collective-permute-start.2
  305.4 5.4 %collective-permute-done.2 = bf16[32,4096]{1,0:T(8,128)(2,1)S(1)} collective-permute-done((bf16[32,4096]{1,0:T(8,128)(2,1)S(1)}, bf16[32,4096]{1,0:T(8,128)(2,1)S(1)}, u32[]{:S(2)}, u32[]{:S(2)}) %collective-permute-start.2) | collective-permute-done | bytes 262176 | tf_op jit(solution)/shard_map/ppermute | solution.py:13
  310.7 35.0 %reduce-scatter.11.cloned.1.call-done = bf16[256,1024]{1,0:T(8,128)(2,1)} async-done(((bf16[1024,1024]{1,0:T(8,128)(2,1)}), bf16[256,1024]{1,0:T(8,128)(2,1)}) %reduce-scatter.11.cloned.1.call-update) | async-done | bytes 524304 | tf_op jit(solution)/shard_map/reduce_scatter | solution.py:94
  345.7 2.1 bitcast_convert_fusion
  (87 shorter events, 10.4 us)
Async XLA Ops:
  7.2 16.2 %copy-start = (bf16[1,256,4096]{2,1,0:T(8,128)(2,1)S(1)}, bf16[1,256,4096]{2,1,0:T(8,128)(2,1)}, u32[]{:S(2)}) copy-start(bf16[1,256,4096]{2,1,0:T(8,128)(2,1)} %param.13) | copy-start | bytes 6291460
  7.2 47.8 %reduce-scatter.5.cloned.1.call-start = ((), (), s32[]{:S(2)}) async-start(), calls=%async_computation.4 | async-start | bytes 1310720 | tf_op jit(solution)/shard_map/reduce_scatter | solution.py:72
  8.2 8.9 %copy-start.2 = (bf16[1,1,128,4096]{3,2,1,0:T(8,128)(2,1)S(1)}, bf16[1,1,128,4096]{3,2,1,0:T(8,128)(2,1)}, u32[]{:S(2)}) copy-start(bf16[1,1,128,4096]{3,2,1,0:T(8,128)(2,1)} %param.9) | copy-start | bytes 3145732
  17.1 0.7 copy-start.11
  24.8 68.6 %all-gather.7.cloned.1.call-start = ((), (), s32[]{:S(2)}) async-start(), calls=%async_computation.5 | async-start | bytes 1310720 | tf_op jit(solution)/shard_map/all_gather | solution.py:69
  56.1 8.5 %collective-permute-start = (bf16[32,4096]{1,0:T(8,128)(2,1)S(1)}, bf16[32,4096]{1,0:T(8,128)(2,1)S(1)}, u32[]{:S(2)}, u32[]{:S(2)}) collective-permute-start(bf16[32,4096]{1,0:T(8,128)(2,1)S(1)} %get-tuple-element.3), channel_id=1, source_target_pairs={{0,8},{8,16},{16,24},{1,9},{9,17},{17,25},{2,10},{10,18},{18,26},{... | collective-permute-start | bytes 786440 | tf_op jit(solution)/shard_map/ppermute | solution.py:13
  64.7 0.7 copy-start.7
  65.4 65.1 %reduce-scatter.7.cloned.1.call-start = ((), (), s32[]{:S(2)}) async-start(), calls=%async_computation.6 | async-start | bytes 1310720 | tf_op jit(solution)/shard_map/reduce_scatter | solution.py:72
  93.4 3.2 copy-start.3
  102.2 28.3 %copy-start.8 = (bf16[32,4096]{1,0:T(8,128)(2,1)S(1)}, bf16[32,4096]{1,0:T(8,128)(2,1)}, u32[]{:S(2)}) copy-start(bf16[32,4096]{1,0:T(8,128)(2,1)} %copy-done.7) | copy-start | bytes 786436
  103.7 65.2 %all-gather.9.cloned.1.call-start = ((), (), s32[]{:S(2)}) async-start(), calls=%async_computation.7 | async-start | bytes 1310720 | tf_op jit(solution)/shard_map/all_gather | solution.py:69
  131.6 8.6 %collective-permute-start.1 = (bf16[32,4096]{1,0:T(8,128)(2,1)S(1)}, bf16[32,4096]{1,0:T(8,128)(2,1)S(1)}, u32[]{:S(2)}, u32[]{:S(2)}) collective-permute-start(bf16[32,4096]{1,0:T(8,128)(2,1)S(1)} %get-tuple-element.5), channel_id=1, source_target_pairs={{0,8},{8,16},{16,24},{1,9},{9,17},{17,25},{2,10},{10,18},{18,26},{... | collective-permute-start | bytes 786440 | tf_op jit(solution)/shard_map/ppermute | solution.py:13
  140.2 0.7 copy-start.5
  140.9 65.1 %reduce-scatter.9.cloned.1.call-start = ((), (), s32[]{:S(2)}) async-start(), calls=%async_computation.8 | async-start | bytes 1310720 | tf_op jit(solution)/shard_map/reduce_scatter | solution.py:72
  168.9 3.2 copy-start.4
  177.7 28.3 %copy-start.6 = (bf16[32,4096]{1,0:T(8,128)(2,1)S(1)}, bf16[32,4096]{1,0:T(8,128)(2,1)}, u32[]{:S(2)}) copy-start(bf16[32,4096]{1,0:T(8,128)(2,1)} %copy-done.5) | copy-start | bytes 786436
  179.2 28.3 %copy-start.9 = (f32[4096]{0:T(1024)S(1)}, f32[4096]{0:T(1024)}, u32[]{:S(2)}) copy-start(f32[4096]{0:T(1024)} %param.14) | copy-start | bytes 49156
  179.2 38.0 %all-gather.11.cloned.1.call-start = ((), (), s32[]{:S(2)}) async-start(), calls=%async_computation.10 | async-start | bytes 2359296 | tf_op jit(solution)/shard_map/all_gather | solution.py:82
  208.8 82.5 %all-gather.13.cloned.1.call-start = ((), (), s32[]{:S(2)}) async-start(), calls=%async_computation.11 | async-start | bytes 7864320 | tf_op jit(solution)/shard_map/all_gather | solution.py:18
  208.8 9.9 %copy-start.1 = (bf16[1,3,2,32,1024]{4,3,2,1,0:T(8,128)(2,1)S(1)}, bf16[1,3,2,32,1024]{4,3,2,1,0:T(8,128)(2,1)}, u32[]{:S(2)}) copy-start(bf16[1,3,2,32,1024]{4,3,2,1,0:T(8,128)(2,1)} %param.15) | copy-start | bytes 1179652
  208.8 10.5 %copy-start.10 = (f32[1,1024]{1,0:T(1,128)S(1)}, f32[1,1024]{1,0:T(1,128)}, u32[]{:S(2)}) copy-start(f32[1,1024]{1,0:T(1,128)} %param.16) | copy-start | bytes 12292
  218.5 127.3 %reduce-scatter.11.cloned.1.call-start = ((), (), s32[]{:S(2)}) async-start(), calls=%async_computation.9 | async-start | bytes 2621440 | tf_op jit(solution)/shard_map/reduce_scatter | solution.py:94
  302.0 8.8 %collective-permute-start.2 = (bf16[32,4096]{1,0:T(8,128)(2,1)S(1)}, bf16[32,4096]{1,0:T(8,128)(2,1)S(1)}, u32[]{:S(2)}, u32[]{:S(2)}) collective-permute-start(bf16[32,4096]{1,0:T(8,128)(2,1)S(1)} %get-tuple-element.7), channel_id=1, source_target_pairs={{0,8},{8,16},{16,24},{1,9},{9,17},{17,25},{2,10},{10,18},{18,26},{... | collective-permute-start | bytes 786440 | tf_op jit(solution)/shard_map/ppermute | solution.py:13
Sparse Core Ops, SparseCore 0:
  25.0 29.9 reduce-scatter.4
  65.5 27.8 all-gather.6
  103.8 26.6 reduce-scatter.6
  141.0 27.8 all-gather.8
  179.3 26.6 reduce-scatter.8
  208.9 8.2 all-gather.10
  219.0 72.1 all-gather.12
  302.1 43.6 reduce-scatter.10
